TPU v7x, 32 devices: a whole 2x2x4 slice. The times are simulated.
32 devices in a mesh: row: 4 (over y, core), col: 8 (over z, x).
Axes of the slice: x: 2, y: 2, z: 4, core: 2. Of those that a mesh axis runs over, the one named last changes fastest.
Arguments:
- normal: float32 [16, 4, 256, 8, 8, 256], P(None, 'row', None, None, 'col'), may hold values from -1.5 to 1.5
- panel_inverse: float32 [256, 256], replicated, as said below
- rhs: float32 [16, 4, 256, 512], P(None, 'row', None, 'col'), may hold values from -0.009765625 to 0.009765625
- shifts: float32 [4], replicated, may hold values from 16 to 128
Outputs:
- schur: float32 [16, 4, 256, 8, 8, 256], P(None, 'row', None, None, 'col')
- eliminated: float32 [16, 4, 256, 512], P(None, 'row', None, 'col')
- applied: float32 [16, 4, 256, 512], P(None, 'row', None, 'col')
Inputs may be any that keep to these rules, and one draw needn't show every extreme that they name: `panel_inverse`: lower triangular with positive diagonal entries.
All inputs are finite; a program needn't handle non-finite values.
Results may differ from a plain program's by a relative error of at most 0.000076.
Values sent between devices are 32-bit elements; how exact they have to be, the bound alone decides.
A program may use at most 256 MiB of HBM per device.

v0:
```python
import jax
import jax.numpy as jnp
from jax import lax
from jax.sharding import PartitionSpec as P

R = 128


def spread_2(value, axis, source):
    kept = jnp.where(lax.axis_index(axis) == source, value, 0).astype(value.dtype)
    return lax.psum(kept, axis)


def pick_blocks(blocks, spacing, offset):
    grouped = blocks.reshape((blocks.shape[0] // spacing, spacing) + blocks.shape[1:])
    return lax.dynamic_index_in_dim(grouped, offset, 1, keepdims=False)


def shards(normal, panel_inverse, rhs, shifts):
    high = lax.Precision.HIGHEST
    row_index = lax.axis_index("row")
    col_index = lax.axis_index("col")
    nrow = lax.axis_size("row")
    ncol = lax.axis_size("col")
    spacing = ncol // nrow
    brows, nb, bcols = (normal.shape[0], normal.shape[2], normal.shape[3])
    narrow = rhs.shape[3]
    wide = narrow * ncol
    tile = normal.reshape(brows * nb, bcols * nb)
    owner = col_index % nrow
    offset = col_index // nrow
    local_panel = jnp.dot(
        tile[:, :nb], panel_inverse.T, precision=high, preferred_element_type=jnp.float32
    )
    panel = spread_2(local_panel, "col", 0)
    chosen = pick_blocks(panel.reshape(brows, nb, nb), spacing, offset)
    crossed = spread_2(chosen, "row", owner).reshape(bcols * nb, nb)
    updated = tile - jnp.dot(panel, crossed.T, precision=high, preferred_element_type=jnp.float32)
    leading = spread_2(rhs[0, 0], "row", 0)
    first = jnp.dot(panel_inverse, leading, precision=high, preferred_element_type=jnp.float32)
    reduced = rhs.reshape(brows * nb, narrow) - jnp.dot(
        panel, first, precision=high, preferred_element_type=jnp.float32
    )
    reduced = reduced.reshape(brows, nb, narrow)
    reduced = reduced.at[0].set(jnp.where(row_index == 0, first, reduced[0]))
    spread = lax.all_gather(reduced, "col", axis=2, tiled=True)
    scales = lax.dynamic_slice_in_dim(jnp.repeat(shifts, R), col_index * narrow, narrow)
    partial_value = lax.dot_general(
        updated,
        spread.reshape(brows * nb, wide),
        (((0,), (0,)), ((), ())),
        precision=high,
        preferred_element_type=jnp.float32,
    )
    totals = lax.psum(partial_value, "row")
    totals = totals.reshape(bcols, nb, ncol, narrow)
    arrived = lax.all_to_all(totals, "col", split_axis=2, concat_axis=2, tiled=True)
    arrived = arrived.reshape(bcols, nb, spacing, nrow, narrow)
    arrived = lax.dynamic_index_in_dim(arrived, row_index, 3, keepdims=False)
    product = jnp.transpose(arrived, (0, 2, 1, 3)).reshape(brows, nb, narrow)
    applied = product + reduced * scales[None, None, :]
    schur = updated.reshape(brows, 1, nb, bcols, 1, nb)
    return (schur, reduced.reshape(brows, 1, nb, narrow), applied.reshape(brows, 1, nb, narrow))


def solution(mesh):
    in_specs = (P(None, "row", None, None, "col", None), P(), P(None, "row", None, "col"), P())
    out_specs = (
        P(None, "row", None, None, "col", None),
        P(None, "row", None, "col"),
        P(None, "row", None, "col"),
    )
    return jax.shard_map(shards, mesh=mesh, in_specs=in_specs, out_specs=out_specs, check_vma=False)
```

profile of v0, /device:TPU:0, one launch (start us, length us, event | category | flops | bytes accessed | tf_op | source)
XLA Modules:
  0.0 758.9 jit_solution(6350466244515718778)
XLA Ops:
  7.2 93.9 %reduce.2 = f32[16,256,8,256]{3,2,1,0:T(8,128)} reduce(f32[16,1,256,8,1,256]{5,4,3,2,1,0:T(1,128)} %param.6, f32[]{:T(128)} %constant.77), dimensions={1,4}, to_apply=%param.6.reduce_sub_computation | reduce | bytes 67108864 | tf_op args[0]
  101.1 29.9 %copy.37 = f32[512,8,8,256]{3,1,2,0:T(8,128)} copy(f32[512,8,8,256]{3,2,1,0:T(8,128)} %bitcast.49) | data formatting | bytes 67108864
  131.1 7.7 %convolution_select_fusion = f32[4096,256]{1,0:T(8,128)} fusion(f32[256,256]{1,0:T(8,128)S(1)} %copy-done, f32[4096,2048]{1,0:T(8,128)} %bitcast.47, pred[]{:T(512)S(6)} %eq.12), kind=kOutput, calls=%fused_computation.1 | convolution fusion | flops 3222274048 | bytes 8650753 | tf_op jit(solution)/shard_map/dot_general | solution.py:32
  138.8 1.1 copy-done.5
  140.6 157.4 %all-reduce.5.cloned.1.call-done = f32[4096,256]{1,0:T(8,128)} async-done(((f32[4096,256]{1,0:T(8,128)}), f32[4096,256]{1,0:T(8,128)}) %all-reduce.5.cloned.1.call-update) | async-done | bytes 4194320 | tf_op jit(solution)/shard_map/psum | solution.py:11
  298.0 3.1 dynamic-slice_select_fusion
  301.7 51.0 %all-reduce.9.cloned.1.call-done = (f32[2048,256]{1,0:T(8,128)}, f32[256,64]{0,1:T(8,128)}) async-done(((f32[2048,256]{1,0:T(8,128)}, f32[256,64]{0,1:T(8,128)}), (f32[2048,256]{1,0:T(8,128)}, f32[256,64]{0,1:T(8,128)})) %all-reduce.9.cloned.1.call-update) | async-done | bytes 2162704 | tf_op jit(solution)/shard_map/psum | solution.py:11
  352.7 1.2 fusion.3
  354.0 6.5 convolution_subtract_fusion.1
  360.9 0.9 scatter.4
  361.8 1.0 copy-done.2
  362.9 34.1 %convolution_subtract_fusion = f32[4096,2048]{1,0:T(8,128)} fusion(f32[4096,2048]{1,0:T(8,128)} %bitcast.48, f32[4096,256]{1,0:T(8,128)} %all-reduce.5.cloned.1.call-done, f32[2048,256]{1,0:T(8,128)S(1)} %copy-done.4), kind=kOutput, calls=%fused_computation | convolution fusion | flops 25778192384 | bytes 73400320 | tf_op jit(solution)/shard_map/dot_general | solution.py:38
  397.0 90.5 %all-gather.2.cloned.1.call-done = f32[16,256,512]{1,0,2:T(8,128)} async-done(((f32[16,256,64]{1,0,2:T(8,128)}), f32[16,256,512]{1,0,2:T(8,128)}) %all-gather.2.cloned.1.call-update) | async-done | bytes 8388624 | tf_op jit(solution)/shard_map/all_gather | solution.py:46
  487.5 9.9 %copy.28 = f32[16,256,512]{2,1,0:T(8,128)} copy(f32[16,256,512]{1,0,2:T(8,128)} %all-gather.2.cloned.1.call-done) | data formatting | bytes 16777216 | tf_op jit(solution)/shard_map/all_gather | solution.py:46
  497.4 64.5 %fusion.4 = f32[2048,512]{0,1:T(8,128)S(1)} fusion(f32[4096,2048]{1,0:T(8,128)} %convolution_subtract_fusion, f32[4096,512]{1,0:T(8,128)} %bitcast.55), kind=kOutput, calls=%fused_computation.13 | convolution fusion | flops 51539607552 | bytes 46137344 | tf_op jit(solution)/shard_map/dot_general | solution.py:48
  561.9 4.0 copy.40
  565.9 83.8 %all-reduce.7.cloned.1.call-done = f32[8,256,8,64]{1,0,3,2:T(8,128)} async-done(((f32[8,256,8,64]{1,0,3,2:T(8,128)}), f32[8,256,8,64]{1,0,3,2:T(8,128)}) %all-reduce.7.cloned.1.call-update) | async-done | bytes 4194320 | tf_op jit(solution)/shard_map/psum | solution.py:55
  649.7 5.5 all-to-all-start
  655.4 48.4 %reshape.98 = f32[16,1,256,8,1,256]{5,4,3,2,1,0:T(1,128)} reshape(f32[4096,2048]{1,0:T(8,128)} %convolution_subtract_fusion) | data formatting | bytes 67108864 | tf_op jit(solution)/shard_map/reshape | solution.py:62
  703.8 1.6 copy.33
  705.4 42.8 %all-to-all-done = f32[8,256,8,64]{1,0,3,2:T(8,128)} async-done(((f32[8,256,8,64]{1,0,3,2:T(8,128)}), f32[8,256,8,64]{1,0,3,2:T(8,128)}, u32[]{:S(2)}, u32[]{:S(2)}) %all-to-all-start) | async-done | bytes 4194336 | tf_op jit(solution)/shard_map/all_to_all | solution.py:57
  748.2 1.3 constant_dynamic-slice_fusion
  749.9 0.7 fusion.1
  750.6 1.6 copy.34
  (28 shorter events, 2.3 us)
Async XLA Ops:
  7.2 123.9 %copy-start = (f32[256,256]{1,0:T(8,128)S(1)}, f32[256,256]{1,0:T(8,128)}, u32[]{:S(2)}) copy-start(f32[256,256]{1,0:T(8,128)} %param.7) | copy-start | bytes 786436
  7.2 290.8 %all-reduce.5.cloned.1.call-start = ((), (), s32[]{:S(2)}) async-start(), calls=%async_computation.1 | async-start | bytes 8388608 | tf_op jit(solution)/shard_map/psum | solution.py:11
  138.7 1.2 copy-start.5
  138.7 214.0 %all-reduce.9.cloned.1.call-start = ((), (), s32[]{:S(2)}) async-start(), calls=%async_computation.4 | async-start | bytes 4325376 | tf_op jit(solution)/shard_map/psum | solution.py:11
  301.1 186.4 %all-gather.2.cloned.1.call-start = ((), (), s32[]{:S(2)}) async-start(), calls=%async_computation.2 | async-start | bytes 9437184 | tf_op jit(solution)/shard_map/all_gather | solution.py:46
  354.0 8.9 %copy-start.4 = (f32[2048,256]{1,0:T(8,128)S(1)}, f32[2048,256]{1,0:T(8,128)}, u32[]{:S(2)}) copy-start(f32[2048,256]{1,0:T(8,128)} %get-tuple-element.27) | copy-start | bytes 6291460
  361.8 1.0 copy-start.2
  362.8 286.9 %all-reduce.7.cloned.1.call-start = ((), (), s32[]{:S(2)}) async-start(), calls=%async_computation.3 | async-start | bytes 8388608 | tf_op jit(solution)/shard_map/psum | solution.py:55
  565.9 89.3 %copy-start.6 = (f32[4]{0:T(128)S(1)}, f32[4]{0:T(128)}, u32[]{:S(2)}) copy-start(f32[4]{0:T(128)} %param.9) | copy-start | bytes 52
  649.7 98.5 %all-to-all-start = ((f32[8,256,8,64]{1,0,3,2:T(8,128)}), f32[8,256,8,64]{1,0,3,2:T(8,128)}, u32[]{:S(2)}, u32[]{:S(2)}) async-start(f32[8,256,8,64]{1,0,3,2:T(8,128)} %all-reduce.7.cloned.1.call-done), calls=%async_computation | async-start | bytes 8388608 | tf_op jit(solution)/shard_map/all_to_all | solution.py:57
  655.4 48.4 %copy-start.3 = (f32[16,256,64]{1,0,2:T(8,128)S(1)}, f32[16,256,64]{1,0,2:T(8,128)}, u32[]{:S(2)}) copy-start(f32[16,256,64]{1,0,2:T(8,128)} %copy-done.2) | copy-start | bytes 3145732
  748.2 3.9 copy-start.1
Sparse Core Ops, SparseCore 0:
  138.9 159.0 all-reduce.4
  301.2 51.4 all-reduce.8
  362.9 124.5 all-gather.1
  566.0 83.6 all-reduce.6
where the time goes:
time: 768 us; the launch traced here: 759 us
  waiting for transfers between devices  426 us (55%)
  matrix products  114 us (15%)
  local copies, waits for them, and re-layouts  101 us (13%)
  other arithmetic  98.3 us (13%)
  between operations  14.1 us (2%)
    psum x2, waiting for transfers between devices, spread_2(): return lax.psum(kept, axis)  208 us
    unnamed x1, other arithmetic  93.9 us
    all_gather x1, waiting for transfers between devices, shards(): spread = lax.all_gather(reduced, 'col', axis=2, tiled=True)  90.5 us
    psum x1, waiting for transfers between devices, shards(): totals = lax.psum(partial_value, 'row')  83.8 us
    dot_general x1, matrix products, shards(): lax.dot_general(updated, spread.reshape(brows * nb, wide), (((0,), (0,)),...  64.5 us
    reshape x1, local copies, waits for them, and re-layouts, shards(): schur = updated.reshape(brows, 1, nb, bcols, 1, nb)  48.4 us
    all_to_all x1, waiting for transfers between devices, shards(): lax.all_to_all(totals, 'col', split_axis=2, concat_axis=2, tiled=True)  42.8 us
    unnamed x21, local copies, waits for them, and re-layouts  39.9 us
  transfers between devices with their start and end apart: 5, of which 5 were waited for; matrix products, arithmetic and copies ran while one was open for 11% of the time, Pallas kernels for 0%

commit v1 on v0

--- a/solution.py
+++ b/solution.py
@@ -52,7 +52,9 @@
         precision=high,
         preferred_element_type=jnp.float32,
     )
-    totals = lax.psum(partial_value, "row")
+    totals = partial_value
+    for hop in (1, 2):
+        totals = totals + lax.ppermute(totals, "row", [(dev, dev ^ hop) for dev in range(4)])
     totals = totals.reshape(bcols, nb, ncol, narrow)
     arrived = lax.all_to_all(totals, "col", split_axis=2, concat_axis=2, tiled=True)
     arrived = arrived.reshape(bcols, nb, spacing, nrow, narrow)

time: 768 us -> 792 us (1.031)
  waiting for transfers between devices: 426 us -> 440 us
    ppermute x0 -> x2, waiting for transfers between devices: none -> 98.3 us  [shards(): lax.ppermute(totals, 'row', [(dev, dev ^ hop) for dev in range(4)])]
    psum x1 -> x0, waiting for transfers between devices: 83.8 us -> none  [shards(): totals = lax.psum(partial_value, 'row')]
  transfers between devices with their start and end apart: 5 -> 6, of which waited for: 5 -> 6; matrix products, arithmetic and copies ran while one was open for 11% -> 11% of each run, Pallas kernels for 0% -> 0%
where the time goes in v1:
time: 792 us; the launch traced here: 783 us
  waiting for transfers between devices  440 us (56%)
  matrix products  112 us (14%)
  local copies, waits for them, and re-layouts  108 us (14%)
  other arithmetic  102 us (13%)
  between operations  14.1 us (2%)
    psum x2, waiting for transfers between devices, spread_2(): return lax.psum(kept, axis)  208 us
    ppermute x2, waiting for transfers between devices, shards(): lax.ppermute(totals, 'row', [(dev, dev ^ hop) for dev in range(4)])  98.3 us
    unnamed x1, other arithmetic  93.9 us
    all_gather x1, waiting for transfers between devices, shards(): spread = lax.all_gather(reduced, 'col', axis=2, tiled=True)  90.6 us
    dot_general x1, matrix products, shards(): lax.dot_general(updated, spread.reshape(brows * nb, wide), (((0,), (0,)),...  62.1 us
    reshape x1, local copies, waits for them, and re-layouts, shards(): schur = updated.reshape(brows, 1, nb, bcols, 1, nb)  48.4 us
    all_to_all x1, waiting for transfers between devices, shards(): lax.all_to_all(totals, 'col', split_axis=2, concat_axis=2, tiled=True)  42.7 us
    unnamed x21, local copies, waits for them, and re-layouts  42 us
  transfers between devices with their start and end apart: 6, of which 6 were waited for; matrix products, arithmetic and copies ran while one was open for 11% of the time, Pallas kernels for 0%

profile of v1, /device:TPU:0, one launch (start us, length us, event | category | flops | bytes accessed | tf_op | source)
XLA Modules:
  0.0 783.2 jit_solution(12326741344457682523)
XLA Ops:
  7.2 93.9 %reduce.2 = f32[16,256,8,256]{3,2,1,0:T(8,128)} reduce(f32[16,1,256,8,1,256]{5,4,3,2,1,0:T(1,128)} %param.6, f32[]{:T(128)} %constant.77), dimensions={1,4}, to_apply=%param.6.reduce_sub_computation | reduce | bytes 67108864 | tf_op args[0]
  101.1 29.9 %copy.36 = f32[512,8,8,256]{3,1,2,0:T(8,128)} copy(f32[512,8,8,256]{3,2,1,0:T(8,128)} %bitcast.49) | data formatting | bytes 67108864
  131.1 7.7 convolution_select_fusion
  140.6 157.4 %all-reduce.4.cloned.1.call-done = f32[4096,256]{1,0:T(8,128)} async-done(((f32[4096,256]{1,0:T(8,128)}), f32[4096,256]{1,0:T(8,128)}) %all-reduce.4.cloned.1.call-update) | async-done | bytes 4194320 | tf_op jit(solution)/shard_map/psum | solution.py:11
  298.0 3.1 dynamic-slice_select_fusion
  301.8 51.0 %all-reduce.6.cloned.1.call-done = (f32[2048,256]{1,0:T(8,128)}, f32[256,64]{0,1:T(8,128)}) async-done(((f32[2048,256]{1,0:T(8,128)}, f32[256,64]{0,1:T(8,128)}), (f32[2048,256]{1,0:T(8,128)}, f32[256,64]{0,1:T(8,128)})) %all-reduce.6.cloned.1.call-update) | async-done | bytes 2162704 | tf_op jit(solution)/shard_map/psum | solution.py:11
  352.8 1.2 fusion.3
  354.0 6.5 convolution_subtract_fusion.1
  362.8 34.1 %convolution_subtract_fusion = f32[4096,2048]{1,0:T(8,128)} fusion(f32[4096,2048]{1,0:T(8,128)} %bitcast.48, f32[4096,256]{1,0:T(8,128)} %all-reduce.4.cloned.1.call-done, f32[2048,256]{1,0:T(8,128)S(1)} %copy-done.4), kind=kOutput, calls=%fused_computation | convolution fusion | flops 25778192384 | bytes 73400320 | tf_op jit(solution)/shard_map/dot_general | solution.py:38
  396.9 90.6 %all-gather.2.cloned.1.call-done = f32[16,256,512]{1,0,2:T(8,128)} async-done(((f32[16,256,64]{1,0,2:T(8,128)}), f32[16,256,512]{1,0,2:T(8,128)}) %all-gather.2.cloned.1.call-update) | async-done | bytes 8388624 | tf_op jit(solution)/shard_map/all_gather | solution.py:46
  487.5 9.9 %copy.28 = f32[16,256,512]{2,1,0:T(8,128)} copy(f32[16,256,512]{1,0,2:T(8,128)} %all-gather.2.cloned.1.call-done) | data formatting | bytes 16777216 | tf_op jit(solution)/shard_map/all_gather | solution.py:46
  497.4 62.1 %fusion.4 = f32[2048,512]{1,0:T(8,128)S(1)} fusion(f32[4096,2048]{1,0:T(8,128)} %convolution_subtract_fusion, f32[4096,512]{1,0:T(8,128)} %bitcast.56), kind=kOutput, calls=%fused_computation.13 | convolution fusion | flops 51539607552 | bytes 46137344 | tf_op jit(solution)/shard_map/dot_general | solution.py:48
  559.6 7.1 collective-permute-done
  567.7 1.5 collective-permute-start.1
  569.3 91.1 %collective-permute-done.1 = f32[2048,512]{1,0:T(8,128)S(1)} collective-permute-done((f32[2048,512]{1,0:T(8,128)S(1)}, f32[2048,512]{1,0:T(8,128)S(1)}, u32[]{:S(2)}, u32[]{:S(2)}) %collective-permute-start.1) | collective-permute-done | bytes 4194336 | tf_op jit(solution)/shard_map/ppermute | solution.py:57
  660.4 3.0 add.36
  663.5 5.4 copy.29
  668.9 6.1 copy.39
  675.0 4.7 all-to-all-start
  679.8 48.4 %reshape.98 = f32[16,1,256,8,1,256]{5,4,3,2,1,0:T(1,128)} reshape(f32[4096,2048]{1,0:T(8,128)} %convolution_subtract_fusion) | data formatting | bytes 67108864 | tf_op jit(solution)/shard_map/reshape | solution.py:64
  728.2 1.6 copy.33
  729.8 42.7 %all-to-all-done = f32[8,256,8,64]{1,0,3,2:T(8,128)} async-done(((f32[8,256,8,64]{1,0,3,2:T(8,128)}), f32[8,256,8,64]{1,0,3,2:T(8,128)}, u32[]{:S(2)}, u32[]{:S(2)}) %all-to-all-start) | async-done | bytes 4194336 | tf_op jit(solution)/shard_map/all_to_all | solution.py:59
  772.5 1.3 constant_dynamic-slice_fusion
  774.9 1.6 copy.34
  (32 shorter events, 7.0 us)
Async XLA Ops:
  7.2 123.9 %copy-start = (f32[256,256]{1,0:T(8,128)S(1)}, f32[256,256]{1,0:T(8,128)}, u32[]{:S(2)}) copy-start(f32[256,256]{1,0:T(8,128)} %param.7) | copy-start | bytes 786436
  7.2 290.8 %all-reduce.4.cloned.1.call-start = ((), (), s32[]{:S(2)}) async-start(), calls=%async_computation.1 | async-start | bytes 8388608 | tf_op jit(solution)/shard_map/psum | solution.py:11
  138.7 1.2 copy-start.5
  138.7 214.0 %all-reduce.6.cloned.1.call-start = ((), (), s32[]{:S(2)}) async-start(), calls=%async_computation.3 | async-start | bytes 4325376 | tf_op jit(solution)/shard_map/psum | solution.py:11
  301.1 186.4 %all-gather.2.cloned.1.call-start = ((), (), s32[]{:S(2)}) async-start(), calls=%async_computation.2 | async-start | bytes 9437184 | tf_op jit(solution)/shard_map/all_gather | solution.py:46
  354.0 8.8 %copy-start.4 = (f32[2048,256]{1,0:T(8,128)S(1)}, f32[2048,256]{1,0:T(8,128)}, u32[]{:S(2)}) copy-start(f32[2048,256]{1,0:T(8,128)} %get-tuple-element.27) | copy-start | bytes 6291460
  361.8 1.0 copy-start.2
  559.5 7.2 collective-permute-start
  567.7 92.7 %collective-permute-start.1 = (f32[2048,512]{1,0:T(8,128)S(1)}, f32[2048,512]{1,0:T(8,128)S(1)}, u32[]{:S(2)}, u32[]{:S(2)}) collective-permute-start(f32[2048,512]{1,0:T(8,128)S(1)} %add.35), channel_id=1, source_target_pairs={{0,16},{8,24},{16,0},{24,8},{1,17},{9,25},{17,1},{25,9},{2,18},{10... | collective-permute-start | bytes 12582920 | tf_op jit(solution)/shard_map/ppermute | solution.py:57
  675.0 4.7 copy-start.6
  675.0 97.6 %all-to-all-start = ((f32[8,256,8,64]{1,0,3,2:T(8,128)}), f32[8,256,8,64]{1,0,3,2:T(8,128)}, u32[]{:S(2)}, u32[]{:S(2)}) async-start(f32[8,256,8,64]{1,0,3,2:T(8,128)} %bitcast.51), calls=%async_computation | async-start | bytes 8388608 | tf_op jit(solution)/shard_map/all_to_all | solution.py:59
  679.8 48.4 %copy-start.3 = (f32[16,256,64]{1,0,2:T(8,128)S(1)}, f32[16,256,64]{1,0,2:T(8,128)}, u32[]{:S(2)}) copy-start(f32[16,256,64]{1,0,2:T(8,128)} %copy-done.2) | copy-start | bytes 3145732
  772.5 3.9 copy-start.1
Sparse Core Ops, SparseCore 0:
  138.9 159.1 all-reduce.3
  301.3 51.4 all-reduce.5
  362.9 124.5 all-gather.1
